TPU v7x, 512 devices: a whole 4x4x16 slice. The times are simulated.
512 devices in a mesh: eb: 64 (over y, z), col: 8 (over x, core).
Axes of the slice: x: 4, y: 4, z: 16, core: 2. Of those that a mesh axis runs over, the one named last changes fastest.
Arguments:
- g_lesser: float32 [8, 768, 64, 2, 256], P('col', 'eb'), may hold values from -6 to 6
- g_greater: float32 [8, 768, 64, 2, 256], P('col', 'eb'), may hold values from -6 to 6
- owner_tiles: int32 [8, 768], P('col', 'eb'), may hold values from 0 to 512, as said below
- energy_map: int32 [64], replicated, may hold values from 0 to 63, each once
- coulomb: float32 [8, 2, 256, 256], P('col'), may hold values from -0.21875 to 0.21875
Outputs:
- screened: float32 [64, 8, 2, 2, 256, 256], P('eb', 'col')
Inputs may be any that keep to these rules, and one draw needn't show every extreme that they name: `owner_tiles`: row c lists the tiles of column group c held by each index of eb in 12 consecutive slots; every tile 0 to 511 appears exactly once in the row, 512 marks an empty slot, and in every draw some index of eb holds exactly 12 tiles. `energy_map`: each energy appears exactly once.
All inputs are finite; a program needn't handle non-finite values.
Results may differ from a plain program's by a relative error of at most 0.00007.
Values sent between devices are 32-bit elements; how exact they have to be, the bound alone decides.
No kernel may reach another device: no remote copies, remote signals or barrier semaphores. Data moves between devices by JAX's collectives and lax.ppermute only.
A program may use at most 64 MiB of HBM per device.

v0:
```python
import math

import jax
import jax.numpy as jnp
from jax import lax
from jax.sharding import PartitionSpec as P

precise = lax.Precision.HIGHEST


def extended(value, sides, width):
    for axis, dim in sides:
        devices, length = (lax.axis_size(axis), value.shape[dim])
        up = [(i, (i + 1) % devices) for i in range(devices)]
        down = [(j, i) for i, j in up]
        last = lax.slice_in_dim(value, length - width, length, axis=dim)
        first = lax.slice_in_dim(value, 0, width, axis=dim)
        before = lax.ppermute(last, axis, up)
        after = lax.ppermute(first, axis, down)
        value = jnp.concatenate([before, value, after], axis=dim)
    return value


def left_product(coupling, blocks):
    return jnp.einsum("cab,ecrbd->ecrad", coupling, blocks, precision=precise)


def left_transposed(coupling, blocks):
    return jnp.einsum("cba,ecrbd->ecrad", coupling, blocks, precision=precise)


def right_product(blocks, coupling):
    return jnp.einsum("ecrab,cbd->ecrad", blocks, coupling, precision=precise)


def right_transposed(blocks, coupling):
    return jnp.einsum("ecrab,cdb->ecrad", blocks, coupling, precision=precise)


def upper_blocks(lower):
    flipped = jnp.swapaxes(lower, -1, -2)
    return jnp.stack([-flipped[:, :, 0], flipped[:, :, 1]], axis=2)


def screened_columns(
    diag_prev,
    lower_prev,
    diag_here,
    lower_here,
    diag_next,
    lower_next,
    vl_prev,
    vd_here,
    vl_here,
    vd_next,
    vl_next,
):
    upper_prev = upper_blocks(lower_prev)
    upper_here = upper_blocks(lower_here)
    z_above = right_transposed(diag_prev, vl_prev) + right_transposed(upper_prev, vd_here)
    z_middle = (
        right_transposed(lower_prev, vl_prev)
        + right_transposed(diag_here, vd_here)
        + right_product(upper_here, vl_here)
    )
    z_below = right_transposed(lower_here, vd_here) + right_product(diag_next, vl_here)
    z_farther = right_product(lower_next, vl_here)
    y_diag = (
        left_product(vl_prev, z_above)
        + left_product(vd_here, z_middle)
        + left_transposed(vl_here, z_below)
    )
    y_lower = (
        left_product(vl_here, z_middle)
        + left_product(vd_next, z_below)
        + left_transposed(vl_next, z_farther)
    )
    return jnp.stack([y_diag, y_lower], axis=2)


def body(g_lesser, g_greater, owner_tiles, energy_map, coulomb):
    n_energy = g_lesser.shape[2]
    order_b = g_lesser.shape[4]
    col_local = coulomb.shape[0]
    tile_total = 2 * col_local * order_b
    padded_len = 2 * n_energy
    freq_index = jnp.arange(padded_len, dtype=jnp.int32)
    energy_index = jnp.arange(n_energy, dtype=jnp.int32)
    angle_step = 2.0 * math.pi / padded_len
    fwd_angle = (freq_index[:, None] * energy_index[None, :] % padded_len).astype(
        jnp.float32
    ) * angle_step
    forward = jnp.concatenate([jnp.cos(fwd_angle), jnp.sin(fwd_angle)], axis=0)
    inv_angle = (energy_map[:, None] * freq_index[None, :] % padded_len).astype(
        jnp.float32
    ) * angle_step
    backward = jnp.concatenate([jnp.cos(inv_angle), jnp.sin(inv_angle)], axis=0) / padded_len
    spec_less = jnp.einsum("kn,sncb->skcb", forward, g_lesser[0], precision=precise)
    spec_more = jnp.einsum("kn,sncb->skcb", forward, g_greater[0], precision=precise)
    less_real = spec_less[:, :padded_len, 0] + spec_less[:, padded_len:, 1]
    less_imag = spec_less[:, :padded_len, 1] - spec_less[:, padded_len:, 0]
    more_real = spec_more[:, :padded_len, 0] + spec_more[:, padded_len:, 1]
    more_imag = spec_more[:, :padded_len, 1] - spec_more[:, padded_len:, 0]
    cross = jnp.stack(
        [
            less_real * more_real + less_imag * more_imag,
            less_imag * more_real - less_real * more_imag,
        ],
        axis=2,
    )
    series = jnp.einsum("wk,skcb->swcb", backward, cross, precision=precise)
    corr_real = series[:, :n_energy, 0] - series[:, n_energy:, 1]
    corr_imag = series[:, :n_energy, 1] + series[:, n_energy:, 0]
    factor = 1.0 / math.sqrt(n_energy)
    polar = jnp.stack([corr_imag * factor, -corr_real * factor], axis=2)
    tile_lists = lax.all_gather(owner_tiles, "eb", axis=1, tiled=True)
    arrived = lax.all_to_all(polar, "eb", split_axis=1, concat_axis=0, tiled=True)
    e_local = arrived.shape[1]
    placed = (
        jnp.zeros((tile_total + 1,) + arrived.shape[1:], jnp.float32)
        .at[tile_lists[0]]
        .set(arrived)[:tile_total]
    )
    blocks = placed.reshape(col_local, 2, order_b, e_local, 2, order_b).transpose(3, 0, 1, 4, 2, 5)
    coupling_cycle = extended(coulomb, (("col", 0),), 1)
    vd_here = coulomb[:, 0]
    vl_here = coulomb[:, 1]
    vl_prev = coupling_cycle[:col_local, 1]
    vd_next = coupling_cycle[2:, 0]
    vl_next = coupling_cycle[2:, 1]
    diag_here = blocks[:, :, 0]
    lower_here = blocks[:, :, 1]
    polar_cycle = extended(blocks, (("col", 1),), 1)
    diag_prev = polar_cycle[:, :col_local, 0]
    lower_prev = polar_cycle[:, :col_local, 1]
    diag_next = polar_cycle[:, 2:, 0]
    lower_next = polar_cycle[:, 2:, 1]
    screened = screened_columns(
        diag_prev,
        lower_prev,
        diag_here,
        lower_here,
        diag_next,
        lower_next,
        vl_prev,
        vd_here,
        vl_here,
        vd_next,
        vl_next,
    )
    return screened


def solution(mesh):
    placed = (
        P("col", "eb", None, None, None),
        P("col", "eb", None, None, None),
        P("col", "eb"),
        P(),
        P("col", None, None, None),
    )
    return jax.shard_map(
        body,
        mesh=mesh,
        in_specs=placed,
        out_specs=P("eb", "col", None, None, None, None),
        check_vma=False,
    )
```

profile of v0, /device:TPU:64, one launch (start us, length us, event | category | flops | bytes accessed | tf_op | source)
XLA Modules:
  0.0 207.4 jit_solution(16255734672717541126)
XLA Ops:
  0.0 0.0 copy-start
  0.0 0.1 fusion.69
  0.2 1.3 copy-done
  1.4 0.0 copy-start.2
  1.4 5.1 %convolution_bitcast_fusion = f32[12,256,2,256]{3,1,2,0:T(8,128)S(1)} fusion(f32[12,64,2,256]{3,2,1,0:T(2,128)S(1)} %bitcast.150, f32[128,64]{0,1:T(8,128)S(1)} %get-tuple-element.15, f32[128,64]{0,1:T(8,128)S(1)} %get-tuple-element.16), kind=kOutput, calls=%fused_computation.5 | convolution fusion | flops 1207975936 | bytes 7929856 | tf_op jit(solution)/shard_map/kn,sncb->skcb/dot_general | solution.py:99
  6.5 0.0 copy-done.2
  6.5 0.0 copy-start.3
  6.6 5.1 %convolution_bitcast_fusion.1 = f32[12,256,2,256]{3,1,2,0:T(8,128)S(1)} fusion(f32[12,64,2,256]{3,2,1,0:T(2,128)S(1)} %bitcast.157, f32[128,64]{0,1:T(8,128)S(1)} %get-tuple-element.15, f32[128,64]{0,1:T(8,128)S(1)} %get-tuple-element.16), kind=kOutput, calls=%fused_computation.6 | convolution fusion | flops 1207975936 | bytes 7929856 | tf_op jit(solution)/shard_map/kn,sncb->skcb/dot_general | solution.py:98
  11.7 0.0 copy-done.3
  11.7 0.2 fusion.68
  11.9 1.4 multiply_add_fusion
  13.3 3.3 %fusion.4 = f32[12,128,2,256]{3,1,2,0:T(8,128)S(1)} fusion(f32[12,128,1,256]{3,1,2,0:T(8,128)S(1)} %get-tuple-element.6, f32[12,128,1,256]{3,1,2,0:T(8,128)S(1)} %get-tuple-element.5, f32[64,128]{1,0:T(8,128)S(1)} %get-tuple-element.14, f32[64,128]{1,0:T(8,128)S(1)} %get-tuple-element.13), kind=kOutput, calls=%fused_computation.7 | convolution fusion | flops 1208778752 | bytes 6356992 | tf_op jit(solution)/shard_map/wk,skcb->swcb/dot_general | solution.py:111
  16.6 0.2 fusion.15
  16.8 0.1 pad_maximum_fusion
  16.9 2.4 %copy.46 = f32[12,64,2,256]{3,2,0,1:T(2,128)} copy(f32[12,64,2,256]{3,1,2,0:T(8,128)S(1)} %pad_maximum_fusion) | data formatting | bytes 3145728 | tf_op jit(solution)/shard_map/stack | solution.py:115
  19.3 0.0 copy-start.1
  19.3 0.0 copy-start.4
  19.3 18.2 %all-to-all-start = ((f32[12,64,2,256]{3,2,0,1:T(2,128)}), f32[12,64,2,256]{3,2,0,1:T(2,128)}, u32[]{:S(2)}, u32[]{:S(2)}) async-start(f32[12,64,2,256]{3,2,0,1:T(2,128)} %copy.46), calls=%async_computation | async-start | bytes 3145728 | tf_op jit(solution)/shard_map/all_to_all | solution.py:117
  37.5 0.0 copy-done.1
  37.5 0.0 collective-permute-start.1
  37.5 2.9 %collective-permute-start.3 = (f32[1,2,256,256]{3,2,1,0:T(8,128)S(1)}, f32[1,2,256,256]{3,2,1,0:T(8,128)}, u32[]{:S(2)}, u32[]{:S(2)}) collective-permute-start(f32[1,2,256,256]{3,2,1,0:T(8,128)S(1)} %copy-done.1), channel_id=1, source_target_pairs={{1,0},{2,1},{3,2},{4,3},{5,4},{6,5},{7,6},{0,7},{9,8},{10,9},{11,1... | collective-permute-start | bytes 1572872 | tf_op jit(solution)/shard_map/ppermute | solution.py:19
  40.5 1.3 dynamic-slice
  42.4 0.0 copy-done.4
  42.4 0.1 bitcast_dynamic-update-slice_fusion
  42.5 86.7 %all-reduce = s32[768]{0:T(1024)S(1)} all-reduce(s32[768]{0:T(1024)S(1)} %bitcast_dynamic-update-slice_fusion), channel_id=1, replica_groups=mesh['eb'=64,'col'=8] {'eb'}, use_global_device_ids=true, to_apply=%add | all-reduce | flops 768 | bytes 6144
  129.2 0.0 all-to-all-done
  129.2 0.3 broadcast.36
  129.5 46.1 %scatter_fusion = f32[513,2,256]{2,1,0:T(2,128)S(1)} fusion(f32[513,2,256]{2,1,0:T(2,128)S(1)} %broadcast.36, s32[768]{0:T(1024)S(1)} %fusion.71, f32[768,2,256]{2,1,0:T(2,128)} %bitcast.14), kind=kCustom, calls=%fused_computation | custom fusion | bytes 4721664 | tf_op jit(solution)/shard_map/scatter | solution.py:122
  175.6 0.4 slice.125
  175.9 0.1 copy.75
  176.0 0.0 collective-permute-start
  176.1 2.9 %collective-permute-start.2 = (f32[1,1,2,2,256,256]{5,4,3,2,1,0:T(8,128)S(1)}, f32[1,1,2,2,256,256]{5,4,3,2,1,0:T(8,128)S(1)}, u32[]{:S(2)}, u32[]{:S(2)}) collective-permute-start(f32[1,1,2,2,256,256]{5,4,3,2,1,0:T(8,128)S(1)} %bitcast.152), channel_id=1, source_target_pairs={{1,0},{2,1},{3,2},{4,3},{5,4},{6,5},{7,6},{0,7},{9,8},{10,9},{11,1... | collective-permute-start | bytes 3145736 | tf_op jit(solution)/shard_map/ppermute | solution.py:19
  179.1 0.6 fusion.24
  179.7 0.6 fusion.17
  180.3 1.0 fusion.21
  181.3 10.1 %collective-permute-done = f32[1,1,2,2,256,256]{5,4,3,2,1,0:T(8,128)S(1)} collective-permute-done((f32[1,1,2,2,256,256]{5,4,3,2,1,0:T(8,128)S(1)}, f32[1,1,2,2,256,256]{5,4,3,2,1,0:T(8,128)S(1)}, u32[]{:S(2)}, u32[]{:S(2)}) %collective-permute-start) | collective-permute-done | bytes 1048608 | tf_op jit(solution)/shard_map/ppermute | solution.py:18
  191.6 0.0 collective-permute-done.1
  191.6 1.6 fusion.10
  193.2 1.0 fusion.37
  194.2 1.0 fusion.30
  195.3 0.0 collective-permute-done.2
  195.3 0.6 convolution_add_fusion.2
  195.9 1.0 fusion.32
  196.9 1.0 fusion.18
  197.9 0.6 fusion.16
  198.5 1.6 convolution_add_fusion.5
  200.0 0.0 collective-permute-done.3
  200.1 2.0 convolution_add_fusion.1
  202.0 2.0 fusion.9
  204.0 2.0 fusion.12
  206.0 0.1 pad_maximum_fusion.1
  206.1 1.3 copy.57
  (6 shorter events, 0.2 us)
Async XLA Ops:
  0.0 1.4 copy-start
  1.4 5.1 %copy-start.2 = (f32[1,12,64,2,256]{4,3,2,1,0:T(2,128)S(1)}, f32[1,12,64,2,256]{4,3,2,1,0:T(2,128)}, u32[]{:S(2)}) copy-start(f32[1,12,64,2,256]{4,3,2,1,0:T(2,128)} %param.5) | copy-start | bytes 4718596
  6.5 5.1 %copy-start.3 = (s32[64]{0:T(128)S(1)}, s32[64]{0:T(128)}, u32[]{:S(2)}) copy-start(s32[64]{0:T(128)} %param.8) | copy-start | bytes 772
  19.3 18.2 %copy-start.1 = (f32[1,2,256,256]{3,2,1,0:T(8,128)S(1)}, f32[1,2,256,256]{3,2,1,0:T(8,128)}, u32[]{:S(2)}) copy-start(f32[1,2,256,256]{3,2,1,0:T(8,128)} %param.9) | copy-start | bytes 1572868
  19.3 23.1 %copy-start.4 = (s32[1,12]{1,0:T(1,128)S(1)}, s32[1,12]{1,0:T(1,128)}, u32[]{:S(2)}) copy-start(s32[1,12]{1,0:T(1,128)} %param.7) | copy-start | bytes 148
  19.3 110.0 %all-to-all-start = ((f32[12,64,2,256]{3,2,0,1:T(2,128)}), f32[12,64,2,256]{3,2,0,1:T(2,128)}, u32[]{:S(2)}, u32[]{:S(2)}) async-start(f32[12,64,2,256]{3,2,0,1:T(2,128)} %copy.46), calls=%async_computation | async-start | bytes 3145728 | tf_op jit(solution)/shard_map/all_to_all | solution.py:117
  37.5 154.1 %collective-permute-start.1 = (f32[1,2,256,256]{3,2,1,0:T(8,128)S(1)}, f32[1,2,256,256]{3,2,1,0:T(8,128)}, u32[]{:S(2)}, u32[]{:S(2)}) collective-permute-start(f32[1,2,256,256]{3,2,1,0:T(8,128)S(1)} %copy-done.1), channel_id=1, source_target_pairs={{0,1},{1,2},{2,3},{3,4},{4,5},{5,6},{6,7},{7,0},{8,9},{9,10},{10,1... | collective-permute-start | bytes 1572872 | tf_op jit(solution)/shard_map/ppermute | solution.py:18
  37.5 162.5 %collective-permute-start.3 = (f32[1,2,256,256]{3,2,1,0:T(8,128)S(1)}, f32[1,2,256,256]{3,2,1,0:T(8,128)}, u32[]{:S(2)}, u32[]{:S(2)}) collective-permute-start(f32[1,2,256,256]{3,2,1,0:T(8,128)S(1)} %copy-done.1), channel_id=1, source_target_pairs={{1,0},{2,1},{3,2},{4,3},{5,4},{6,5},{7,6},{0,7},{9,8},{10,9},{11,1... | collective-permute-start | bytes 1572872 | tf_op jit(solution)/shard_map/ppermute | solution.py:19
  176.0 15.4 %collective-permute-start = (f32[1,1,2,2,256,256]{5,4,3,2,1,0:T(8,128)S(1)}, f32[1,1,2,2,256,256]{5,4,3,2,1,0:T(8,128)S(1)}, u32[]{:S(2)}, u32[]{:S(2)}) collective-permute-start(f32[1,1,2,2,256,256]{5,4,3,2,1,0:T(8,128)S(1)} %bitcast.151), channel_id=1, source_target_pairs={{0,1},{1,2},{2,3},{3,4},{4,5},{5,6},{6,7},{7,0},{8,9},{9,10},{10,1... | collective-permute-start | bytes 3145736 | tf_op jit(solution)/shard_map/ppermute | solution.py:18
  176.1 19.2 %collective-permute-start.2 = (f32[1,1,2,2,256,256]{5,4,3,2,1,0:T(8,128)S(1)}, f32[1,1,2,2,256,256]{5,4,3,2,1,0:T(8,128)S(1)}, u32[]{:S(2)}, u32[]{:S(2)}) collective-permute-start(f32[1,1,2,2,256,256]{5,4,3,2,1,0:T(8,128)S(1)} %bitcast.152), channel_id=1, source_target_pairs={{1,0},{2,1},{3,2},{4,3},{5,4},{6,5},{7,6},{0,7},{9,8},{10,9},{11,1... | collective-permute-start | bytes 3145736 | tf_op jit(solution)/shard_map/ppermute | solution.py:19
where the time goes:
time: 211 us; the launch traced here: 207 us
  blocking collectives  86.7 us (41%)
  local copies, waits for them, and re-layouts  53.2 us (25%)
  matrix products  30 us (14%)
  starting transfers between devices  24.1 us (11%)
  waiting for transfers between devices  10.1 us (5%)
  other arithmetic  2.22 us (1%)
    unnamed x1, blocking collectives  86.7 us
    scatter x1, local copies, waits for them, and re-layouts, body(): placed = jnp.zeros((tile_total + 1,) + arrived.shape[1:], jnp.float32).at...  46.1 us
    all_to_all x1, starting transfers between devices, body(): lax.all_to_all(polar, 'eb', split_axis=1, concat_axis=0, tiled=True)  18.2 us
    ppermute x2, waiting for transfers between devices, extended(): before = lax.ppermute(last, axis, up)  10.1 us
    dot_general x4, matrix products, left_product(): return jnp.einsum('cab,ecrbd->ecrad', coupling, blocks, precision=precise)  5.98 us
    ppermute x2, starting transfers between devices, extended(): after = lax.ppermute(first, axis, down)  5.89 us
    dot_general x5, matrix products, right_transposed(): return jnp.einsum('ecrab,cdb->ecrad', blocks, coupling, precision=precise)  5.43 us
    dot_general x1, matrix products, body(): jnp.einsum('kn,sncb->skcb', forward, g_lesser[0], precision=precise)  5.12 us
  transfers between devices with their start and end apart: 5, of which 1 were waited for; matrix products, arithmetic and copies ran while one was open for 28% of the time, Pallas kernels for 0%

commit v1 on v0

v1 whole, which is shorter than its diff:
```python
import math

import jax
import jax.numpy as jnp
import numpy as np
from jax import lax
from jax.experimental import pallas as pl
from jax.experimental.pallas import tpu as pltpu
from jax.sharding import PartitionSpec as P

f32 = jnp.float32
bf16 = jnp.bfloat16
LANES = 128


def halves(x):
    high = x.astype(bf16)
    low = (x - high.astype(f32)).astype(bf16)
    return high, low


def product(a, b):
    (ah, al), (bh, bl) = a, b
    dot = lambda u, v: jnp.dot(u, v, preferred_element_type=f32)
    return dot(ah, bh) + (dot(ah, bl) + dot(al, bh))


def transform_tables(n_energy):
    padded = 2 * n_energy
    k = np.arange(padded)
    n = np.arange(n_energy)
    angle = 2.0 * np.pi * (np.outer(k, n) % padded) / padded
    c, s = np.cos(angle), np.sin(angle)
    forward = np.block([[c, s], [-s, c]])
    scale = 1.0 / (padded * math.sqrt(n_energy))
    backward = np.block([[s.T, c.T], [-c.T, s.T]]) * scale
    return forward.astype(np.float32), backward.astype(np.float32)


def numpy_halves(x):
    high = x.astype(bf16)
    low = (x - high.astype(np.float32)).astype(bf16)
    return high, low


def correlate_kernel(
    slots, step_slots, n_energy, n_dest, stride,
    tiles_ref, emap_ref, fh_ref, fl_ref, bh_ref, bl_ref, less_ref, more_ref,
    out_ref, backh, backl,
):
    step = pl.program_id(0)

    @pl.when(step == 0)
    def _():
        row = jnp.broadcast_to(emap_ref[...], (n_dest, n_energy))
        i0 = lax.broadcasted_iota(jnp.int32, (n_dest, n_energy), 0)
        i1 = lax.broadcasted_iota(jnp.int32, (n_dest, n_energy), 1)
        column = jnp.sum(jnp.where(i0 == i1, row, 0), axis=1, keepdims=True)
        pick = jnp.where(i1 == column, 1.0, 0.0).astype(bf16)
        for part in range(2):
            rows = slice(part * n_energy, (part + 1) * n_energy)
            dest = slice(part * n_dest, (part + 1) * n_dest)
            for source, target in ((bh_ref, backh), (bl_ref, backl)):
                target[dest, :] = jnp.dot(
                    pick, source[rows, :], preferred_element_type=f32
                ).astype(bf16)
        lane = lax.broadcasted_iota(jnp.int32, (1, LANES), 1)
        ids = jnp.zeros((1, LANES), jnp.int32)
        for s in range(slots):
            ids = jnp.where(lane == s, tiles_ref[0, s], ids)
        out_ref[pl.ds(stride - 1, n_dest, stride=stride), :] = jnp.broadcast_to(
            ids.astype(f32), (n_dest, LANES)
        )

    forward = (fh_ref[...], fl_ref[...])
    backward = (backh[...], backl[...])

    def spectrum(ref, i):
        piece = lambda q: ref[i, pl.ds(q, n_energy, stride=4), :]
        re = jnp.concatenate([piece(0), piece(2)], axis=1)
        im = jnp.concatenate([piece(1), piece(3)], axis=1)
        return product(forward, halves(jnp.concatenate([re, im], axis=0)))

    for i in range(step_slots):
        less = spectrum(less_ref, i)
        more = spectrum(more_ref, i)
        half = 2 * n_energy
        lr, li, mr, mi = less[:half], less[half:], more[:half], more[half:]
        cross = jnp.concatenate([lr * mr + li * mi, li * mr - lr * mi], axis=0)
        series = product(backward, halves(cross))
        slot = step * step_slots + i
        for q in range(4):
            value = series[(q // 2) * n_dest:(q // 2 + 1) * n_dest,
                           (q % 2) * LANES:(q % 2 + 1) * LANES]
            out_ref[pl.ds(slot * 4 + q, n_dest, stride=stride), :] = value


def correlate(less, more, tiles, emap, n_dest, interpret=False):
    slots, n_energy = less.shape[0], less.shape[1]
    stride = slots * 4 + 1
    step_slots = 2
    forward, backward = transform_tables(n_energy)
    tables = numpy_halves(forward) + numpy_halves(backward)

    def packed(x):
        x = x.reshape(slots, n_energy, 2, 2, LANES).transpose(0, 1, 3, 2, 4)
        return x.reshape(slots, n_energy * 4, LANES)

    whole = lambda shape: pl.BlockSpec(shape, lambda i: (0,) * len(shape))
    slot_block = pl.BlockSpec((step_slots, n_energy * 4, LANES), lambda i: (i, 0, 0))
    kernel = lambda *refs: correlate_kernel(
        slots, step_slots, n_energy, n_dest, stride, *refs
    )
    return pl.pallas_call(
        kernel,
        grid=(slots // step_slots,),
        in_specs=[
            pl.BlockSpec(memory_space=pltpu.SMEM),
            whole((1, n_energy)),
            whole(tables[0].shape), whole(tables[1].shape),
            whole(tables[2].shape), whole(tables[3].shape),
            slot_block, slot_block,
        ],
        out_specs=whole((n_dest * stride, LANES)),
        out_shape=jax.ShapeDtypeStruct((n_dest * stride, LANES), f32),
        scratch_shapes=[
            pltpu.VMEM((2 * n_dest, 4 * n_energy), bf16),
            pltpu.VMEM((2 * n_dest, 4 * n_energy), bf16),
        ],
        interpret=interpret,
    )(tiles, emap.reshape(1, n_energy), *[jnp.asarray(t) for t in tables],
      packed(less), packed(more))


def place_kernel(slots, n_source, order, group, in_ref, out_ref):
    stride = slots * 4 + 1
    ids = in_ref[pl.ds(stride - 1, n_source, stride=stride), :]
    by_slot = jnp.transpose(ids)
    total_h = total_l = None
    for g in range(0, slots, group):
        row = jnp.concatenate([by_slot[s:s + 1, :] for s in range(g, g + group)], axis=1)
        width = group * n_source
        tile = lax.broadcasted_iota(jnp.int32, (2 * order, width), 0).astype(f32)
        pick = jnp.where(tile == row, 1.0, 0.0).astype(bf16)
        values = jnp.concatenate(
            [
                jnp.concatenate(
                    [in_ref[pl.ds(s * 4 + q, n_source, stride=stride), :] for q in range(4)],
                    axis=1,
                )
                for s in range(g, g + group)
            ],
            axis=0,
        )
        high, low = halves(values)
        h = jnp.dot(pick, high, preferred_element_type=f32)
        l = jnp.dot(pick, low, preferred_element_type=f32)
        total_h = h if total_h is None else total_h + h
        total_l = l if total_l is None else total_l + l
    dense = total_h + total_l
    out_ref[0, :, :] = dense[:, :order]
    out_ref[1, :, :] = dense[:, order:]


def place(arrived, slots, n_source, order, interpret=False):
    kernel = lambda *refs: place_kernel(slots, n_source, order, 4, *refs)
    return pl.pallas_call(
        kernel,
        out_shape=jax.ShapeDtypeStruct((2, 2 * order, order), f32),
        compiler_params=pltpu.CompilerParams(vmem_limit_bytes=32 << 20),
        interpret=interpret,
    )(arrived)


def screen_kernel(order, p_prev, p_here, p_next, v_prev, v_here, v_next, out_ref):
    b = order
    rows = lambda ref: ref[...].reshape(4 * b, b)
    flip = jnp.transpose
    vl_prev, vd, vl = v_prev[1], v_here[0], v_here[1]
    vd_next, vl_next = v_next[0], v_next[1]

    def upper(ref):
        return jnp.concatenate([-flip(ref[0, b:, :]), flip(ref[1, b:, :])], axis=0)

    vd_t, vl_h, vlp_t = halves(flip(vd)), halves(vl), halves(flip(vl_prev))
    from_prev = product(halves(rows(p_prev)), vlp_t)
    from_here = product(halves(rows(p_here)), vd_t)
    from_next = product(halves(rows(p_next)), vl_h)
    up_prev = product(halves(upper(p_prev)), vd_t)
    up_here = product(halves(upper(p_here)), vl_h)

    def beside(x, block):
        return jnp.concatenate(
            [x[block * b:(block + 1) * b], x[(2 + block) * b:(3 + block) * b]], axis=1
        )

    def pair(x):
        return jnp.concatenate([x[:b], x[b:]], axis=1)

    above = beside(from_prev, 0) + pair(up_prev)
    middle = beside(from_prev, 1) + beside(from_here, 0) + pair(up_here)
    below = beside(from_here, 1) + beside(from_next, 0)
    farther = beside(from_next, 1)
    stack = lambda *x: jnp.concatenate(x, axis=0)
    side = lambda *x: jnp.concatenate(x, axis=1)
    above, middle, below, farther = map(halves, (above, middle, below, farther))
    column = lambda *z: tuple(stack(*part) for part in zip(*z))
    diag = product(halves(side(vl_prev, vd, flip(vl))), column(above, middle, below))
    lower = product(halves(side(vl, vd_next, flip(vl_next))), column(middle, below, farther))
    for k, value in ((0, diag), (1, lower)):
        out_ref[k, 0, :, :] = value[:, :b]
        out_ref[k, 1, :, :] = value[:, b:]


def screen(p_prev, p_here, p_next, v_prev, v_here, v_next, interpret=False):
    b = v_here.shape[-1]
    kernel = lambda *refs: screen_kernel(b, *refs)
    return pl.pallas_call(
        kernel,
        out_shape=jax.ShapeDtypeStruct((2, 2, b, b), f32),
        compiler_params=pltpu.CompilerParams(vmem_limit_bytes=48 << 20),
        interpret=interpret,
    )(p_prev, p_here, p_next, v_prev, v_here, v_next)


def from_neighbours(value, axis):
    devices = lax.axis_size(axis)
    up = [(i, (i + 1) % devices) for i in range(devices)]
    down = [(j, i) for i, j in up]
    return lax.ppermute(value, axis, up), lax.ppermute(value, axis, down)


def body(g_lesser, g_greater, owner_tiles, energy_map, coulomb):
    slots, order = g_lesser.shape[1], g_lesser.shape[4]
    n_eb = lax.axis_size("eb")
    v_here = coulomb[0]
    v_prev, v_next = from_neighbours(v_here, "col")
    sent = correlate(g_lesser[0], g_greater[0], owner_tiles, energy_map, n_eb)
    sent, v_prev, v_next = lax.optimization_barrier((sent, v_prev, v_next))
    arrived = lax.all_to_all(
        sent.reshape(n_eb, 1, -1), "eb", split_axis=0, concat_axis=0, tiled=True
    )
    p_here = place(arrived.reshape(-1, LANES), slots, n_eb, order)
    p_prev, p_next = from_neighbours(p_here, "col")
    return screen(p_prev, p_here, p_next, v_prev, v_here, v_next)[None, None]


def solution(mesh):
    placed = (
        P("col", "eb", None, None, None),
        P("col", "eb", None, None, None),
        P("col", "eb"),
        P(),
        P("col", None, None, None),
    )
    return jax.shard_map(
        body,
        mesh=mesh,
        in_specs=placed,
        out_specs=P("eb", "col", None, None, None, None),
        check_vma=False,
    )
```

time: 211 us -> 132 us (0.63)
  the two profiles are of different devices: /device:TPU:64 before, /device:TPU:16 now
where the time goes in v1:
time: 132 us; the launch traced here: 131 us
  blocking collectives  94.9 us (72%)
  Pallas kernels  16.7 us (13%)
  waiting for transfers between devices  16.4 us (12%)
  starting transfers between devices  3.3 us (2%)
    all_to_all x1, blocking collectives, body(): lax.all_to_all(sent.reshape(n_eb, 1, -1), 'eb', split_axis=0, concat_axis...  94.9 us
    ppermute x4, waiting for transfers between devices, from_neighbours(): return (lax.ppermute(value, axis, up), lax.ppermute(value, axis, down))  16.4 us
    pallas_call x1, Pallas kernels, correlate(): pl.pallas_call(kernel, grid=(slots // step_slots,), in_specs=[pl.BlockSpe...  9.05 us
    pallas_call x1, Pallas kernels, screen(): pl.pallas_call(kernel, out_shape=jax.ShapeDtypeStruct((2, 2, b, b), f32),...  6.51 us
    ppermute x4, starting transfers between devices, from_neighbours(): return (lax.ppermute(value, axis, up), lax.ppermute(value, axis, down))  3.3 us
  transfers between devices with their start and end apart: 4, of which 3 were waited for; matrix products, arithmetic and copies ran while one was open for 0% of the time, Pallas kernels for 7%

profile of v1, /device:TPU:16, one launch (start us, length us, event | category | flops | bytes accessed | tf_op | source)
XLA Modules:
  0.0 131.3 jit_solution(1806063985457953862)
XLA Ops:
  0.0 2.2 %collective-permute-start.1 = (f32[2,256,256]{2,1,0:T(8,128)}, f32[2,256,256]{2,1,0:T(8,128)S(1)}, u32[]{:S(2)}, u32[]{:S(2)}) collective-permute-start(f32[2,256,256]{2,1,0:T(8,128)} %bitcast.16), channel_id=1, source_target_pairs={{1,0},{2,1},{3,2},{4,3},{5,4},{6,5},{7,6},{0,7},{9,8},{10,9},{11,1... | collective-permute-start | bytes 1572872 | tf_op jit(solution)/shard_map/ppermute | solution.py:230
  2.2 0.0 collective-permute-start
  2.2 9.0 %shard_map.91 = f32[3136,128]{1,0:T(8,128)} custom-call(s32[1,12]{1,0:T(1,128)} %refs_0_.1, s32[1,64]{1,0:T(1,128)} %bitcast.22, bf16[256,128]{1,0:T(8,128)(2,1)} %constant.8.clone.refs_2_, bf16[256,128]{1,0:T(8,128)(2,1)} %constant.9.clone.refs_3_, bf16[128,256]{1,0:T(8,128)(2,1)} %constant.10.clone.refs_4_, bf16[128,256]{1,0:T(8,128)(2,1)} %constant.11.clone.refs_5_, ...), custom_call_target="tpu_custom_call" | custom-call | tf_op jit(solution)/shard_map/pallas_call | solution.py:114
  11.2 0.0 collective-permute-done.1.refs_5_
  11.3 1.0 collective-permute-done.refs_3_
  12.2 94.9 %all_to_all.5 = f32[64,1,6272]{2,1,0:T(1,128)S(1)} all-to-all(f32[64,1,6272]{2,1,0:T(1,128)} %bitcast.19), channel_id=1, replica_groups=mesh['eb'=64,'col'=8] {'eb'}, dimensions={0} | all-to-all | bytes 3211264 | tf_op jit(solution)/shard_map/all_to_all | solution.py:240
  107.2 0.0 copy-start
  107.2 1.1 shard_map.92.refs_1_
  108.3 1.1 collective-permute-start.3
  109.3 0.0 collective-permute-start.2
  109.3 12.3 %collective-permute-done.3.refs_2_ = f32[2,512,256]{2,1,0:T(8,128)S(1)} collective-permute-done((f32[2,512,256]{2,1,0:T(8,128)S(1)}, f32[2,512,256]{2,1,0:T(8,128)S(1)}, u32[]{:S(2)}, u32[]{:S(2)}) %collective-permute-start.3) | collective-permute-done | bytes 1048608 | tf_op jit(solution)/shard_map/ppermute | solution.py:230
  121.7 3.1 %collective-permute-done.2.refs_0_ = f32[2,512,256]{2,1,0:T(8,128)S(1)} collective-permute-done((f32[2,512,256]{2,1,0:T(8,128)S(1)}, f32[2,512,256]{2,1,0:T(8,128)S(1)}, u32[]{:S(2)}, u32[]{:S(2)}) %collective-permute-start.2) | collective-permute-done | bytes 1048608 | tf_op jit(solution)/shard_map/ppermute | solution.py:230
  124.8 0.0 copy-done
  124.8 6.5 %shard_map.93 = f32[2,2,256,256]{3,2,1,0:T(8,128)} custom-call(f32[2,512,256]{2,1,0:T(8,128)S(1)} %collective-permute-done.2.refs_0_, f32[2,512,256]{2,1,0:T(8,128)S(1)} %shard_map.92.refs_1_, f32[2,512,256]{2,1,0:T(8,128)S(1)} %collective-permute-done.3.refs_2_, f32[2,256,256]{2,1,0:T(8,128)S(1)} %collective-permute-done.refs_3_, ...), custom_call_target="tpu_custom_call" | custom-call | tf_op jit(solution)/shard_map/pallas_call | solution.py:218
Async XLA Ops:
  0.0 11.3 %collective-permute-start.1 = (f32[2,256,256]{2,1,0:T(8,128)}, f32[2,256,256]{2,1,0:T(8,128)S(1)}, u32[]{:S(2)}, u32[]{:S(2)}) collective-permute-start(f32[2,256,256]{2,1,0:T(8,128)} %bitcast.16), channel_id=1, source_target_pairs={{1,0},{2,1},{3,2},{4,3},{5,4},{6,5},{7,6},{0,7},{9,8},{10,9},{11,1... | collective-permute-start | bytes 1572872 | tf_op jit(solution)/shard_map/ppermute | solution.py:230
  2.2 10.0 %collective-permute-start = (f32[2,256,256]{2,1,0:T(8,128)}, f32[2,256,256]{2,1,0:T(8,128)S(1)}, u32[]{:S(2)}, u32[]{:S(2)}) collective-permute-start(f32[2,256,256]{2,1,0:T(8,128)} %bitcast.17), channel_id=1, source_target_pairs={{0,1},{1,2},{2,3},{3,4},{4,5},{5,6},{6,7},{7,0},{8,9},{9,10},{10,1... | collective-permute-start | bytes 1572872 | tf_op jit(solution)/shard_map/ppermute | solution.py:230
  107.2 17.6 %copy-start = (f32[1,2,256,256]{3,2,1,0:T(8,128)S(1)}, f32[1,2,256,256]{3,2,1,0:T(8,128)}, u32[]{:S(2)}) copy-start(f32[1,2,256,256]{3,2,1,0:T(8,128)} %param.13) | copy-start | bytes 1572868
  108.3 13.4 %collective-permute-start.3 = (f32[2,512,256]{2,1,0:T(8,128)S(1)}, f32[2,512,256]{2,1,0:T(8,128)S(1)}, u32[]{:S(2)}, u32[]{:S(2)}) collective-permute-start(f32[2,512,256]{2,1,0:T(8,128)S(1)} %shard_map.92.refs_1_), channel_id=1, source_target_pairs={{1,0},{2,1},{3,2},{4,3},{5,4},{6,5},{7,6},{0,7},{9,8},{10,9},{11,1... | collective-permute-start | bytes 3145736 | tf_op jit(solution)/shard_map/ppermute | solution.py:230
  109.3 15.4 %collective-permute-start.2 = (f32[2,512,256]{2,1,0:T(8,128)S(1)}, f32[2,512,256]{2,1,0:T(8,128)S(1)}, u32[]{:S(2)}, u32[]{:S(2)}) collective-permute-start(f32[2,512,256]{2,1,0:T(8,128)S(1)} %shard_map.92.refs_1_), channel_id=1, source_target_pairs={{0,1},{1,2},{2,3},{3,4},{4,5},{5,6},{6,7},{7,0},{8,9},{9,10},{10,1... | collective-permute-start | bytes 3145736 | tf_op jit(solution)/shard_map/ppermute | solution.py:230
